TPU v7x, 32 devices: a whole 2x2x4 slice. The times are simulated.
32 devices in a mesh: tile: 8 (over y, x, core), plane: 4 (over z).
Axes of the slice: x: 2, y: 2, z: 4, core: 2. Of those that a mesh axis runs over, the one named last changes fastest.
Arguments:
- raw_tiles: bfloat16 [4, 64, 2, 16, 1024], P('plane', 'tile'), may hold values from 0.5 to 2.5
- flat_profile: bfloat16 [2, 16, 1024], P(None, 'plane'), may hold values from 0.5 to 1.5
- dark_profile: bfloat16 [2, 16, 1024], P(None, 'plane'), may hold values from 0 to 0.5
- destinations: int32 [4, 64, 1], P('plane', 'tile'), may hold values from 0 to 7, as said below
- positions: int32 [4, 64], P('plane', 'tile'), may hold values from 0 to 31
- levels: int32 [4, 64], P('plane', 'tile'), may hold values from 1 to 4
Outputs:
- stitched: bfloat16 [4, 2, 4096, 1024], P('plane', None, 'tile')
Inputs may be any that keep to these rules, and one draw needn't show every extreme that they name: `destinations`: the owner of a tile acquired by the device at index i of tile (aligned blocks of 8 tiles of a plane) is one of i - 2, ..., i + 2 or i + 4, modulo 8; among one device's tiles no owner is named more than 2 times, some owner exactly 2 times, and the owner i + 4 exactly 2 times.
All inputs are finite; a program needn't handle non-finite values.
Results may differ from a plain program's by a relative error of at most 0.0045.
Values may be sent and summed in bfloat16 or wider, within the bound.
No kernel may reach another device: no remote copies, remote signals or barrier semaphores. Data moves between devices by JAX's collectives and lax.ppermute only.
A program may use at most 64 MiB of HBM per device.

v0:
```python
import jax
import jax.numpy as jnp
from jax import lax
from jax.sharding import PartitionSpec as P

CR = 512
screen_weight = 0.5


def padded(cells, sides, width):
    for axis, dim in sides:
        count = lax.axis_size(axis)
        ends = count - 1
        head = lax.slice_in_dim(cells, 0, width, axis=dim)
        tail = lax.slice_in_dim(cells, cells.shape[dim] - width, cells.shape[dim], axis=dim)
        cells = jnp.concatenate(
            [
                lax.ppermute(tail, axis, [(i, (i + 1) % count) for i in range(ends)]),
                cells,
                lax.ppermute(head, axis, [((i + 1) % count, i) for i in range(ends)]),
            ],
            axis=dim,
        )
    return cells


def ramp_weights(tile_rows):
    tile_row = jnp.arange(tile_rows)
    return jnp.minimum(tile_row + 1, tile_rows - tile_row).astype(jnp.float32)


def apply_weights(camera, flat_full, dark_full, gains):
    corrected = (
        camera.astype(jnp.float32) - dark_full.astype(jnp.float32)[None]
    ) / flat_full.astype(jnp.float32)[None]
    scale = gains[:, None, None, None] * ramp_weights(camera.shape[2])[None, None, :, None]
    return (corrected * scale).astype(jnp.bfloat16)


def neighbour_sum(above, below, middle):
    zero_col = jnp.zeros(middle.shape[:2] + (1,), jnp.float32)
    shifted_left = jnp.concatenate([zero_col, middle[:, :, :-1]], 2)
    shifted_right = jnp.concatenate([middle[:, :, 1:], zero_col], 2)
    return above + below + shifted_left + shifted_right


def per_device(raw_tiles, flat_profile, dark_profile, destinations, positions, levels):
    camera = raw_tiles[0]
    owners = destinations[0, :, 0]
    grid_pos = positions[0]
    gains_int = levels[0]
    tile_count = camera.shape[0]
    tile_rows = camera.shape[2]
    owner_count = lax.axis_size("tile")
    capacity = max(2, tile_count // 4)
    canvas_rows = CR
    my_index = lax.axis_index("tile")
    flat_full, dark_full = (
        lax.all_gather(flat_profile, "plane", axis=1, tiled=True),
        lax.all_gather(dark_profile, "plane", axis=1, tiled=True),
    )
    same_dest = owners[:, None] == owners[None, :]
    earlier = jnp.arange(tile_count)[None, :] < jnp.arange(tile_count)[:, None]
    slot_rank = jnp.sum((same_dest & earlier).astype(jnp.int32), axis=1)
    slot_of = owners * capacity + slot_rank
    slot_total = owner_count * capacity
    matches = (slot_of[None, :] == jnp.arange(slot_total)[:, None]).astype(jnp.int32)
    slot_tile = jnp.sum(matches * jnp.arange(tile_count)[None, :], axis=1)
    occupied = jnp.sum(matches, axis=1)
    slot_gain = jnp.sum(matches * gains_int[None, :], axis=1)
    slot_pos = jnp.sum(matches * grid_pos[None, :], axis=1)
    slot_info = jnp.stack([slot_gain, slot_pos], 1).astype(jnp.bfloat16)
    occupied_mask = occupied.astype(jnp.bfloat16)[:, None, None, None]
    outgoing = jnp.take(camera, slot_tile, axis=0) * occupied_mask
    arrived, arrived_info = (
        lax.all_to_all(outgoing, "tile", split_axis=0, concat_axis=0, tiled=True),
        lax.all_to_all(slot_info, "tile", split_axis=0, concat_axis=0, tiled=True),
    )
    arrived_gain = arrived_info[:, 0].astype(jnp.float32)
    weighted = apply_weights(arrived, flat_full, dark_full, arrived_gain)
    first_rows = arrived_info[:, 1].astype(jnp.int32) * 16
    row_ids = jnp.arange(canvas_rows)[:, None, None]
    covered = row_ids == first_rows[None, :, None] + jnp.arange(tile_rows)[None, None, :]
    placement = covered.astype(jnp.bfloat16)
    accumulated = jnp.einsum(
        "ysr,scrx->cyx", placement, weighted, preferred_element_type=jnp.float32
    )
    row_gain = arrived_gain[:, None] * ramp_weights(tile_rows)[None, :]
    weight_sum = jnp.einsum("ysr,sr->y", covered.astype(jnp.float32), row_gain)
    blended = accumulated / jnp.maximum(weight_sum, 1.0)[None, :, None]
    extended = padded(blended.astype(jnp.bfloat16), (("tile", 1),), 3).astype(blended.dtype)
    global_rows = my_index * canvas_rows - 3 + jnp.arange(canvas_rows + 6)
    inside = ((global_rows >= 0) & (global_rows < owner_count * canvas_rows)).astype(jnp.float32)
    field = extended
    for sweep_id in range(3):
        kept = field.shape[1] - 2
        middle = field[:, 1:-1]
        neighbours = neighbour_sum(field[:, :-2], field[:, 2:], middle)
        source = extended[:, sweep_id + 1 : sweep_id + 1 + kept]
        mask_rows = inside[sweep_id + 1 : sweep_id + 1 + kept][None, :, None]
        field = (screen_weight * source + neighbours) / (screen_weight + 4.0) * mask_rows
    return field.astype(jnp.bfloat16)[None]


def solution(mesh):
    placed = (
        P("plane", "tile", None, None, None),
        P(None, "plane", None),
        P(None, "plane", None),
        P("plane", "tile", None),
        P("plane", "tile"),
        P("plane", "tile"),
    )
    return jax.shard_map(
        per_device,
        mesh=mesh,
        in_specs=placed,
        out_specs=P("plane", None, "tile", None),
        check_vma=False,
    )
```

profile of v0, /device:TPU:3, one launch (start us, length us, event | category | flops | bytes accessed | tf_op | source)
XLA Modules:
  0.0 81.8 jit_solution(9118618087000041648)
XLA Ops:
  0.0 0.0 copy-start
  0.0 0.9 %convert_reduce_fusion.1 = s32[8]{0:T(128)S(1)} fusion(s32[8]{0:T(128)} %bitcast.41), kind=kLoop, calls=%fused_computation.51 | loop fusion | flops 312 | bytes 64 | tf_op jit(solution)/shard_map/reduce_sum | solution.py:64
  0.9 0.7 multiply_add_fusion
  1.6 0.8 convert_reduce_fusion
  2.4 0.1 stack.9
  2.4 0.1 stack.10
  2.5 0.6 copy.27
  3.1 4.5 %all-to-all-start.1 = ((bf16[8,2,2]{1,2,0:T(2,128)(2,1)}), bf16[8,2,2]{1,2,0:T(2,128)(2,1)S(1)}, u32[]{:S(2)}, u32[]{:S(2)}) async-start(bf16[8,2,2]{1,2,0:T(2,128)(2,1)} %copy.27), calls=%async_computation.1 | async-start | bytes 8192 | tf_op jit(solution)/shard_map/all_to_all | solution.py:77
  7.7 0.1 slice_multiply_fusion.3
  7.8 0.1 slice_multiply_fusion.4
  7.9 0.7 copy.25
  8.6 0.7 copy.23
  9.4 10.6 %all_gather.6 = bf16[2,16,1024]{2,0,1:T(2,128)(2,1)S(1)} all-gather(bf16[2,4,1024]{2,0,1:T(2,128)(2,1)S(1)} %copy.23), channel_id=1, replica_groups=mesh['tile'=8,'plane'=4] {'plane'}, dimensions={1}, use_global_device_ids=true | all-gather | bytes 81920 | tf_op jit(solution)/shard_map/all_gather | solution.py:60
  20.0 10.2 %all_gather.7 = bf16[2,16,1024]{2,0,1:T(2,128)(2,1)S(1)} all-gather(bf16[2,4,1024]{2,0,1:T(2,128)(2,1)S(1)} %copy.25), channel_id=1, replica_groups=mesh['tile'=8,'plane'=4] {'plane'}, dimensions={1}, use_global_device_ids=true | all-gather | bytes 81920 | tf_op jit(solution)/shard_map/all_gather | solution.py:59
  30.2 0.0 copy-done
  30.2 0.6 gather_fusion
  30.9 1.2 %select_multiply_fusion = bf16[16,2,16,1024]{3,2,1,0:T(8,128)(2,1)} fusion(bf16[16,2,16,1024]{3,2,1,0:T(8,128)(2,1)S(1)} %gather_fusion, pred[16]{0:T(512)(128)(4,1)S(1)} %compare_and_fusion, bf16[16]{0:T(256)(128)(2,1)S(1)} %convert_element_type.77), kind=kLoop, calls=%fused_computation.29 | loop fusion | flops 1048576 | bytes 2097200 | tf_op jit(solution)/shard_map/mul | solution.py:74
  32.0 0.0 all-to-all-done.1
  32.0 10.0 %all-to-all-start = ((bf16[16,2,16,1024]{3,2,1,0:T(8,128)(2,1)}), bf16[16,2,16,1024]{3,2,1,0:T(8,128)(2,1)S(1)}, u32[]{:S(2)}, u32[]{:S(2)}) async-start(bf16[16,2,16,1024]{3,2,1,0:T(8,128)(2,1)} %select_multiply_fusion), calls=%async_computation | async-start | bytes 2097152 | tf_op jit(solution)/shard_map/all_to_all | solution.py:76
  42.0 0.1 all_to_all.11
  42.1 0.1 iota_add_fusion
  42.2 0.1 broadcast_multiply_fusion
  42.3 0.3 fusion.19
  42.5 13.3 %all-to-all-done = bf16[16,2,16,1024]{3,2,1,0:T(8,128)(2,1)S(1)} async-done(((bf16[16,2,16,1024]{3,2,1,0:T(8,128)(2,1)}), bf16[16,2,16,1024]{3,2,1,0:T(8,128)(2,1)S(1)}, u32[]{:S(2)}, u32[]{:S(2)}) %all-to-all-start) | async-done | bytes 1048608 | tf_op jit(solution)/shard_map/all_to_all | solution.py:76
  55.8 0.9 %fusion.15 = bf16[2,512,1024]{2,1,0:T(8,128)(2,1)S(1)} fusion(f32[512]{0:T(512)S(1)} %broadcast_maximum_fusion, bf16[16,2,16,1024]{3,2,1,0:T(8,128)(2,1)S(1)} %all-to-all-done, f32[16,16]{1,0:T(8,128)S(1)} %broadcast_multiply_fusion, f32[2,16,1024]{2,1,0:T(8,128)S(1)} %copy_convert_fusion, f32[2,16,1024]{2,1,0:T(8,128)S(1)} %copy_convert_fusion.1, ...), kind=kOutput, calls=%fused_computation.25 | convolution fusion | flops 541720576 | bytes 3411968 | tf_op jit(solution)/shard_map/ysr,scrx->cyx/dot_general | solution.py:85
  56.8 3.5 %collective-permute-start = (bf16[2,3,1024]{2,1,0:T(4,128)(2,1)S(1)}, bf16[2,3,1024]{2,1,0:T(4,128)(2,1)S(1)}, u32[]{:S(2)}, u32[]{:S(2)}) collective-permute-start(bf16[2,3,1024]{2,1,0:T(4,128)(2,1)S(1)} %get-tuple-element.15), channel_id=1, source_target_pairs={{0,4},{4,8},{8,12},{12,16},{16,20},{20,24},{24,28},{1,5},{5,9},{9,... | collective-permute-start | bytes 36872 | tf_op jit(solution)/shard_map/ppermute | solution.py:18
  60.2 1.9 %collective-permute-start.1 = (bf16[2,3,1024]{2,1,0:T(4,128)(2,1)S(1)}, bf16[2,3,1024]{2,1,0:T(4,128)(2,1)S(1)}, u32[]{:S(2)}, u32[]{:S(2)}) collective-permute-start(bf16[2,3,1024]{2,1,0:T(4,128)(2,1)S(1)} %get-tuple-element.16), channel_id=1, source_target_pairs={{4,0},{8,4},{12,8},{16,12},{20,16},{24,20},{28,24},{5,1},{9,5},{13... | collective-permute-start | bytes 36872 | tf_op jit(solution)/shard_map/ppermute | solution.py:20
  62.2 0.1 slice_multiply_fusion.5
  62.2 0.0 collective-permute-done
  62.2 4.0 %collective-permute-done.1 = bf16[2,3,1024]{2,1,0:T(4,128)(2,1)S(1)} collective-permute-done((bf16[2,3,1024]{2,1,0:T(4,128)(2,1)S(1)}, bf16[2,3,1024]{2,1,0:T(4,128)(2,1)S(1)}, u32[]{:S(2)}, u32[]{:S(2)}) %collective-permute-start.1) | collective-permute-done | bytes 12320 | tf_op jit(solution)/shard_map/ppermute | solution.py:20
  66.2 0.6 maximum_convert_fusion
  66.8 2.2 %fusion.34 = (f32[2,516,1023]{2,1,0:T(8,128)S(1)}, f32[2,516,1023]{2,1,0:T(8,128)S(1)}) fusion(f32[2,518,1024]{2,1,0:T(8,128)S(1)} %maximum_convert_fusion), kind=kLoop, calls=%fused_computation.71 | loop fusion | bytes 16891776 | tf_op jit(solution)/shard_map/slice | solution.py:42
  69.0 2.5 %fusion.7 = f32[2,516,1024]{2,1,0:T(8,128)S(1)} fusion(f32[2,518,1024]{2,1,0:T(8,128)S(1)} %maximum_convert_fusion, f32[2,516,1023]{2,1,0:T(8,128)S(1)} %get-tuple-element.14, f32[2,516,1023]{2,1,0:T(8,128)S(1)} %get-tuple-element.13, f32[516]{0:T(1024)S(1)} %slice_multiply_fusion.4), kind=kLoop, calls=%fused_computation.10 | loop fusion | flops 6340608 | bytes 25356240 | tf_op jit(solution)/shard_map/mul | solution.py:101
  71.5 2.2 %fusion.33 = (f32[2,514,1023]{2,1,0:T(8,128)S(1)}, f32[2,514,1023]{2,1,0:T(8,128)S(1)}) fusion(f32[2,516,1024]{2,1,0:T(8,128)S(1)} %fusion.7), kind=kLoop, calls=%fused_computation.70 | loop fusion | bytes 16826304 | tf_op jit(solution)/shard_map/slice | solution.py:42
  73.6 2.6 %fusion.3 = f32[2,514,1024]{2,1,0:T(8,128)S(1)} fusion(f32[2,516,1024]{2,1,0:T(8,128)S(1)} %fusion.7, f32[2,518,1024]{2,1,0:T(8,128)S(1)} %maximum_convert_fusion, f32[2,514,1023]{2,1,0:T(8,128)S(1)} %get-tuple-element.12, f32[2,514,1023]{2,1,0:T(8,128)S(1)} %get-tuple-element.11, f32[514]{0:T(1024)S(1)} %slice_multiply_fusion.3), kind=kLoop, calls=%fused_computation.5 | loop fusion | flops 6316032 | bytes 25257960 | tf_op jit(solution)/shard_map/mul | solution.py:101
  76.3 2.1 %fusion.32 = (f32[2,512,1023]{2,1,0:T(8,128)S(1)}, f32[2,512,1023]{2,1,0:T(8,128)S(1)}) fusion(f32[2,514,1024]{2,1,0:T(8,128)S(1)} %fusion.3), kind=kLoop, calls=%fused_computation.69 | loop fusion | bytes 16760832 | tf_op jit(solution)/shard_map/slice | solution.py:42
  78.4 3.5 %fusion.14 = bf16[1,2,512,1024]{3,2,1,0:T(8,128)(2,1)} fusion(f32[512]{0:T(512)S(1)} %slice_multiply_fusion.5, f32[2,512,1023]{2,1,0:T(8,128)S(1)} %get-tuple-element.10, f32[2,512,1023]{2,1,0:T(8,128)S(1)} %get-tuple-element.9, f32[2,514,1024]{2,1,0:T(8,128)S(1)} %fusion.3, f32[2,518,1024]{2,1,0:T(8,128)S(1)} %maximum_convert_fusion), kind=kLoop, calls=%fused_computation.24 | loop fusion | flops 7340032 | bytes 23062528 | tf_op jit(solution)/shard_map/broadcast_in_dim | solution.py:102
  (16 shorter events, 0.1 us)
Async XLA Ops:
  0.0 30.2 %copy-start = (bf16[1,8,2,16,1024]{4,3,2,1,0:T(8,128)(2,1)S(1)}, bf16[1,8,2,16,1024]{4,3,2,1,0:T(8,128)(2,1)}, u32[]{:S(2)}) copy-start(bf16[1,8,2,16,1024]{4,3,2,1,0:T(8,128)(2,1)} %param.6) | copy-start | bytes 1572868
  3.1 28.9 %all-to-all-start.1 = ((bf16[8,2,2]{1,2,0:T(2,128)(2,1)}), bf16[8,2,2]{1,2,0:T(2,128)(2,1)S(1)}, u32[]{:S(2)}, u32[]{:S(2)}) async-start(bf16[8,2,2]{1,2,0:T(2,128)(2,1)} %copy.27), calls=%async_computation.1 | async-start | bytes 8192 | tf_op jit(solution)/shard_map/all_to_all | solution.py:77
  32.0 23.8 %all-to-all-start = ((bf16[16,2,16,1024]{3,2,1,0:T(8,128)(2,1)}), bf16[16,2,16,1024]{3,2,1,0:T(8,128)(2,1)S(1)}, u32[]{:S(2)}, u32[]{:S(2)}) async-start(bf16[16,2,16,1024]{3,2,1,0:T(8,128)(2,1)} %select_multiply_fusion), calls=%async_computation | async-start | bytes 2097152 | tf_op jit(solution)/shard_map/all_to_all | solution.py:76
  56.8 5.5 %collective-permute-start = (bf16[2,3,1024]{2,1,0:T(4,128)(2,1)S(1)}, bf16[2,3,1024]{2,1,0:T(4,128)(2,1)S(1)}, u32[]{:S(2)}, u32[]{:S(2)}) collective-permute-start(bf16[2,3,1024]{2,1,0:T(4,128)(2,1)S(1)} %get-tuple-element.15), channel_id=1, source_target_pairs={{0,4},{4,8},{8,12},{12,16},{16,20},{20,24},{24,28},{1,5},{5,9},{9,... | collective-permute-start | bytes 36872 | tf_op jit(solution)/shard_map/ppermute | solution.py:18
  60.2 6.0 %collective-permute-start.1 = (bf16[2,3,1024]{2,1,0:T(4,128)(2,1)S(1)}, bf16[2,3,1024]{2,1,0:T(4,128)(2,1)S(1)}, u32[]{:S(2)}, u32[]{:S(2)}) collective-permute-start(bf16[2,3,1024]{2,1,0:T(4,128)(2,1)S(1)} %get-tuple-element.16), channel_id=1, source_target_pairs={{4,0},{8,4},{12,8},{16,12},{20,16},{24,20},{28,24},{5,1},{9,5},{13... | collective-permute-start | bytes 36872 | tf_op jit(solution)/shard_map/ppermute | solution.py:20
where the time goes:
time: 82.3 us; the launch traced here: 81.8 us
  blocking collectives  20.8 us (25%)
  starting transfers between devices  19.9 us (24%)
  waiting for transfers between devices  17.2 us (21%)
  other arithmetic  13.1 us (16%)
  local copies, waits for them, and re-layouts  9.41 us (11%)
  matrix products  1.16 us (1%)
    all_to_all x1, waiting for transfers between devices, per_device(): lax.all_to_all(outgoing, 'tile', split_axis=0, concat_axis=0, tiled=True)  13.3 us
    all_gather x1, blocking collectives, per_device(): lax.all_gather(dark_profile, 'plane', axis=1, tiled=True)  10.6 us
    all_gather x1, blocking collectives, per_device(): lax.all_gather(flat_profile, 'plane', axis=1, tiled=True)  10.2 us
    all_to_all x1, starting transfers between devices, per_device(): lax.all_to_all(outgoing, 'tile', split_axis=0, concat_axis=0, tiled=True)  9.97 us
    slice x3, local copies, waits for them, and re-layouts, neighbour_sum(): shifted_left = jnp.concatenate([zero_col, middle[:, :, :-1]], 2)  6.44 us
    mul x5, other arithmetic, per_device(): (screen_weight * source + neighbours) / (screen_weight + 4.0) * mask_rows  5.32 us
    all_to_all x1, starting transfers between devices, per_device(): lax.all_to_all(slot_info, 'tile', split_axis=0, concat_axis=0, tiled=True)  4.53 us
    ppermute x1, waiting for transfers between devices, padded(): lax.ppermute(head, axis, [((i + 1) % count, i) for i in range(ends)])  3.95 us
  transfers between devices with their start and end apart: 4, of which 2 were waited for; matrix products, arithmetic and copies ran while one was open for 5% of the time, Pallas kernels for 0%

commit v1 on v0

--- a/solution.py
+++ b/solution.py
@@ -5,6 +5,22 @@
 
 CR = 512
 screen_weight = 0.5
+
+
+def test_counts_all(content, axis_no, local_values):
+    v_now = content.shape
+    r_now = content.reshape(
+        *v_now[:axis_no], local_values, v_now[axis_no] // local_values, *v_now[axis_no + 1 :]
+    )
+    met_up = jnp.moveaxis(r_now, axis_no, 0)
+    return met_up
+
+
+def wall_end(block_in, join_dim):
+    oldest = list(block_in.shape[1:])
+    oldest[join_dim] *= block_in.shape[0]
+    b_now = jnp.moveaxis(block_in, 0, join_dim).reshape(oldest)
+    return b_now
 
 
 def padded(cells, sides, width):
@@ -72,9 +88,24 @@
     slot_info = jnp.stack([slot_gain, slot_pos], 1).astype(jnp.bfloat16)
     occupied_mask = occupied.astype(jnp.bfloat16)[:, None, None, None]
     outgoing = jnp.take(camera, slot_tile, axis=0) * occupied_mask
+
+    def see_racks(a0, axis_id, panel, arr):
+        later = jax.lax.psum(1, axis_name=axis_id)
+        h_now, outcome_arr = (later, jax.lax.axis_index(axis_id))
+        lower = test_counts_all(a0, panel, h_now)
+        val = lower
+        for to_i in range(1, h_now):
+            v1, aux = ((outcome_arr + to_i) % h_now, (outcome_arr - to_i) % h_now)
+            view_out = lax.dynamic_index_in_dim(lower, v1, 0)
+            seen_now = tuple(((idx, (idx + to_i) % h_now) for idx in range(h_now)))
+            before = jax.lax.ppermute(view_out, axis_name=axis_id, perm=seen_now)
+            val = lax.dynamic_update_slice_in_dim(val, before, aux, axis=0)
+        tmp = wall_end(val, arr)
+        return tmp
+
     arrived, arrived_info = (
         lax.all_to_all(outgoing, "tile", split_axis=0, concat_axis=0, tiled=True),
-        lax.all_to_all(slot_info, "tile", split_axis=0, concat_axis=0, tiled=True),
+        see_racks(slot_info, "tile", 0, 0),
     )
     arrived_gain = arrived_info[:, 0].astype(jnp.float32)
     weighted = apply_weights(arrived, flat_full, dark_full, arrived_gain)

time: 82.3 us -> 76 us (0.923)
  waiting for transfers between devices: 17.2 us -> 6.51 us
  starting transfers between devices: 19.9 us -> 24.7 us
    ppermute x0 -> x7, starting transfers between devices: none -> 13.9 us  [see_racks(): before = jax.lax.ppermute(view_out, axis_name=axis_id, perm=seen_now)]
    all_to_all x1, waiting for transfers between devices: 13.3 us -> 0.01 us  [per_device(): lax.all_to_all(outgoing, 'tile', split_axis=0, concat_axis=0, tiled=True)]
    all_to_all x1, starting transfers between devices: 9.97 us -> 4.2 us  [per_device(): lax.all_to_all(outgoing, 'tile', split_axis=0, concat_axis=0, tiled=True)]
    all_to_all x1 -> x0, starting transfers between devices: 4.53 us -> none  [per_device(): lax.all_to_all(slot_info, 'tile', split_axis=0, concat_axis=0, tiled=True)]
    ppermute x0 -> x7, waiting for transfers between devices: none -> 2.73 us  [see_racks(): before = jax.lax.ppermute(view_out, axis_name=axis_id, perm=seen_now)]
    unnamed x4 -> x8, local copies, waits for them, and re-layouts: 1.47 us -> 0.04 us
    dynamic_update_slice x0 -> x8, local copies, waits for them, and re-layouts: none -> 1.23 us  [see_racks(): val = lax.dynamic_update_slice_in_dim(val, before, aux, axis=0)]
    ppermute x1, starting transfers between devices: 3.47 us -> 4.55 us  [padded(): lax.ppermute(tail, axis, [(i, (i + 1) % count) for i in range(ends)])]
  transfers between devices with their start and end apart: 4 -> 10, of which waited for: 2 -> 3; matrix products, arithmetic and copies ran while one was open for 5% -> 5% of each run, Pallas kernels for 0% -> 0%
where the time goes in v1:
time: 76 us; the launch traced here: 75.8 us
  starting transfers between devices  24.7 us (32%)
  blocking collectives  20.8 us (27%)
  other arithmetic  13.4 us (18%)
  local copies, waits for them, and re-layouts  8.8 us (12%)
  waiting for transfers between devices  6.51 us (9%)
  matrix products  1.16 us (2%)
    ppermute x7, starting transfers between devices, see_racks(): before = jax.lax.ppermute(view_out, axis_name=axis_id, perm=seen_now)  13.9 us
    all_gather x1, blocking collectives, per_device(): lax.all_gather(dark_profile, 'plane', axis=1, tiled=True)  10.6 us
    all_gather x1, blocking collectives, per_device(): lax.all_gather(flat_profile, 'plane', axis=1, tiled=True)  10.2 us
    slice x3, local copies, waits for them, and re-layouts, neighbour_sum(): shifted_left = jnp.concatenate([zero_col, middle[:, :, :-1]], 2)  6.44 us
    mul x5, other arithmetic, per_device(): (screen_weight * source + neighbours) / (screen_weight + 4.0) * mask_rows  5.31 us
    ppermute x1, starting transfers between devices, padded(): lax.ppermute(tail, axis, [(i, (i + 1) % count) for i in range(ends)])  4.55 us
    all_to_all x1, starting transfers between devices, per_device(): lax.all_to_all(outgoing, 'tile', split_axis=0, concat_axis=0, tiled=True)  4.2 us
    ppermute x1, waiting for transfers between devices, padded(): lax.ppermute(head, axis, [((i + 1) % count, i) for i in range(ends)])  3.77 us
  transfers between devices with their start and end apart: 10, of which 3 were waited for; matrix products, arithmetic and copies ran while one was open for 5% of the time, Pallas kernels for 0%

profile of v1, /device:TPU:3, one launch (start us, length us, event | category | flops | bytes accessed | tf_op | source)
XLA Modules:
  0.0 75.8 jit_solution(7785738213039110962)
XLA Ops:
  0.0 0.0 copy-start
  0.0 0.0 copy-start.1
  0.0 0.0 copy-start.2
  0.1 0.9 %convert_reduce_fusion.1 = s32[8]{0:T(128)S(1)} fusion(s32[8]{0:T(128)} %bitcast.41), kind=kLoop, calls=%fused_computation.50 | loop fusion | flops 312 | bytes 64 | tf_op jit(solution)/shard_map/reduce_sum | solution.py:80
  1.0 0.7 multiply_add_fusion
  1.6 0.8 convert_reduce_fusion
  2.4 0.1 stack.9
  2.5 0.1 copy.27
  2.6 0.1 stack.10
  2.7 0.1 copy.28
  2.8 0.1 fusion.34
  2.9 0.1 collective-permute-start.5
  3.0 2.3 %collective-permute-start.2 = (bf16[1,2,2]{0,2,1:T(2,128)(2,1)S(1)}, bf16[1,2,2]{0,2,1:T(2,128)(2,1)S(1)}, u32[]{:S(2)}, u32[]{:S(2)}) collective-permute-start(bf16[1,2,2]{0,2,1:T(2,128)(2,1)S(1)} %get-tuple-element.21), channel_id=1, source_target_pairs={{0,12},{4,16},{8,20},{12,24},{16,28},{20,0},{24,4},{28,8},{1,13},{... | collective-permute-start | bytes 32 | tf_op jit(solution)/shard_map/ppermute | solution.py:101
  5.3 0.0 collective-permute-start.3
  5.3 0.1 fusion.35
  5.4 2.0 %collective-permute-start.6 = (bf16[1,2,2]{0,2,1:T(2,128)(2,1)S(1)}, bf16[1,2,2]{0,2,1:T(2,128)(2,1)S(1)}, u32[]{:S(2)}, u32[]{:S(2)}) collective-permute-start(bf16[1,2,2]{0,2,1:T(2,128)(2,1)S(1)} %get-tuple-element.17), channel_id=1, source_target_pairs={{0,28},{4,0},{8,4},{12,8},{16,12},{20,16},{24,20},{28,24},{1,29},{... | collective-permute-start | bytes 32 | tf_op jit(solution)/shard_map/ppermute | solution.py:101
  7.4 0.7 collective-permute-start
  8.1 0.0 copy-done
  8.1 0.6 gather_fusion
  8.7 1.2 %select_multiply_fusion = bf16[16,2,16,1024]{3,2,1,0:T(8,128)(2,1)} fusion(bf16[16,2,16,1024]{3,2,1,0:T(8,128)(2,1)S(1)} %gather_fusion, pred[16]{0:T(512)(128)(4,1)S(1)} %compare_and_fusion, bf16[16]{0:T(256)(128)(2,1)S(1)} %convert_element_type.77), kind=kLoop, calls=%fused_computation.29 | loop fusion | flops 1048576 | bytes 2097200 | tf_op jit(solution)/shard_map/mul | solution.py:90
  9.9 4.2 %all-to-all-start = ((bf16[16,2,16,1024]{3,2,1,0:T(8,128)(2,1)}), bf16[16,2,16,1024]{3,2,1,0:T(8,128)(2,1)S(1)}, u32[]{:S(2)}, u32[]{:S(2)}) async-start(bf16[16,2,16,1024]{3,2,1,0:T(8,128)(2,1)} %select_multiply_fusion), calls=%async_computation | async-start | bytes 2097152 | tf_op jit(solution)/shard_map/all_to_all | solution.py:107
  14.1 0.1 slice_multiply_fusion.3
  14.2 0.1 slice_multiply_fusion.4
  14.3 0.1 fusion.33
  14.4 0.0 copy-done.1
  14.4 0.0 copy-done.2
  14.4 10.6 %all_gather.6 = bf16[2,16,1024]{2,0,1:T(2,128)(2,1)S(1)} all-gather(bf16[2,4,1024]{2,0,1:T(2,128)(2,1)S(1)} %copy.23), channel_id=1, replica_groups=mesh['tile'=8,'plane'=4] {'plane'}, dimensions={1}, use_global_device_ids=true | all-gather | bytes 81920 | tf_op jit(solution)/shard_map/all_gather | solution.py:76
  25.0 10.2 %all_gather.7 = bf16[2,16,1024]{2,0,1:T(2,128)(2,1)S(1)} all-gather(bf16[2,4,1024]{2,0,1:T(2,128)(2,1)S(1)} %copy.25), channel_id=1, replica_groups=mesh['tile'=8,'plane'=4] {'plane'}, dimensions={1}, use_global_device_ids=true | all-gather | bytes 81920 | tf_op jit(solution)/shard_map/all_gather | solution.py:75
  35.3 0.0 collective-permute-done
  35.3 1.2 %collective-permute-start.1 = (bf16[1,2,2]{0,2,1:T(2,128)(2,1)S(1)}, bf16[1,2,2]{0,2,1:T(2,128)(2,1)S(1)}, u32[]{:S(2)}, u32[]{:S(2)}) collective-permute-start(bf16[1,2,2]{0,2,1:T(2,128)(2,1)S(1)} %get-tuple-element.19), channel_id=1, source_target_pairs={{0,8},{4,12},{8,16},{12,20},{16,24},{20,28},{24,0},{28,4},{1,9},{5... | collective-permute-start | bytes 32 | tf_op jit(solution)/shard_map/ppermute | solution.py:101
  36.6 0.2 dynamic_update_slice.21
  36.8 1.4 %collective-permute-done.1 = bf16[1,2,2]{0,2,1:T(2,128)(2,1)S(1)} collective-permute-done((bf16[1,2,2]{0,2,1:T(2,128)(2,1)S(1)}, bf16[1,2,2]{0,2,1:T(2,128)(2,1)S(1)}, u32[]{:S(2)}, u32[]{:S(2)}) %collective-permute-start.1) | collective-permute-done | bytes 40 | tf_op jit(solution)/shard_map/ppermute | solution.py:101
  38.1 7.5 %collective-permute-start.4 = (bf16[1,2,2]{0,2,1:T(2,128)(2,1)S(1)}, bf16[1,2,2]{0,2,1:T(2,128)(2,1)S(1)}, u32[]{:S(2)}, u32[]{:S(2)}) collective-permute-start(bf16[1,2,2]{0,2,1:T(2,128)(2,1)S(1)} %fusion.33), channel_id=1, source_target_pairs={{0,20},{4,24},{8,28},{12,0},{16,4},{20,8},{24,12},{28,16},{1,21},{... | collective-permute-start | bytes 32 | tf_op jit(solution)/shard_map/ppermute | solution.py:101
  45.7 0.2 dynamic_update_slice.22
  45.8 0.0 collective-permute-done.2
  45.9 0.0 collective-permute-done.3
  45.9 0.2 dynamic_update_slice.24
  46.1 1.4 %collective-permute-done.4 = bf16[1,2,2]{0,2,1:T(2,128)(2,1)S(1)} collective-permute-done((bf16[1,2,2]{0,2,1:T(2,128)(2,1)S(1)}, bf16[1,2,2]{0,2,1:T(2,128)(2,1)S(1)}, u32[]{:S(2)}, u32[]{:S(2)}) %collective-permute-start.4) | collective-permute-done | bytes 40 | tf_op jit(solution)/shard_map/ppermute | solution.py:101
  47.5 0.2 dynamic_update_slice.25
  47.6 0.0 collective-permute-done.5
  47.7 0.2 dynamic_update_slice.26
  47.9 0.0 collective-permute-done.6
  47.9 0.2 dynamic_update_slice.27
  48.1 0.1 copy.29
  48.2 0.1 reshape.135
  48.3 0.1 iota_add_fusion
  48.3 0.1 broadcast_multiply_fusion
  48.4 0.3 fusion.19
  48.7 0.0 all-to-all-done
  48.7 0.9 %fusion.15 = bf16[2,512,1024]{2,1,0:T(8,128)(2,1)S(1)} fusion(f32[512]{0:T(512)S(1)} %broadcast_maximum_fusion, bf16[16,2,16,1024]{3,2,1,0:T(8,128)(2,1)S(1)} %all-to-all-done, f32[16,16]{1,0:T(8,128)S(1)} %broadcast_multiply_fusion, f32[2,16,1024]{2,1,0:T(8,128)S(1)} %copy_convert_fusion, f32[2,16,1024]{2,1,0:T(8,128)S(1)} %copy_convert_fusion.1, ...), kind=kOutput, calls=%fused_computation.25 | convolution fusion | flops 541720576 | bytes 3411968 | tf_op jit(solution)/shard_map/ysr,scrx->cyx/dot_general | solution.py:116
  49.6 4.5 %collective-permute-start.7 = (bf16[2,3,1024]{2,1,0:T(4,128)(2,1)S(1)}, bf16[2,3,1024]{2,1,0:T(4,128)(2,1)S(1)}, u32[]{:S(2)}, u32[]{:S(2)}) collective-permute-start(bf16[2,3,1024]{2,1,0:T(4,128)(2,1)S(1)} %get-tuple-element.15), channel_id=1, source_target_pairs={{0,4},{4,8},{8,12},{12,16},{16,20},{20,24},{24,28},{1,5},{5,9},{9,... | collective-permute-start | bytes 36872 | tf_op jit(solution)/shard_map/ppermute | solution.py:34
  54.2 2.1 %collective-permute-start.8 = (bf16[2,3,1024]{2,1,0:T(4,128)(2,1)S(1)}, bf16[2,3,1024]{2,1,0:T(4,128)(2,1)S(1)}, u32[]{:S(2)}, u32[]{:S(2)}) collective-permute-start(bf16[2,3,1024]{2,1,0:T(4,128)(2,1)S(1)} %get-tuple-element.16), channel_id=1, source_target_pairs={{4,0},{8,4},{12,8},{16,12},{20,16},{24,20},{28,24},{5,1},{9,5},{13... | collective-permute-start | bytes 36872 | tf_op jit(solution)/shard_map/ppermute | solution.py:36
  56.3 0.1 slice_multiply_fusion.5
  56.4 0.0 collective-permute-done.7
  56.4 3.8 %collective-permute-done.8 = bf16[2,3,1024]{2,1,0:T(4,128)(2,1)S(1)} collective-permute-done((bf16[2,3,1024]{2,1,0:T(4,128)(2,1)S(1)}, bf16[2,3,1024]{2,1,0:T(4,128)(2,1)S(1)}, u32[]{:S(2)}, u32[]{:S(2)}) %collective-permute-start.8) | collective-permute-done | bytes 12320 | tf_op jit(solution)/shard_map/ppermute | solution.py:36
  60.1 0.6 maximum_convert_fusion
  60.8 2.2 %fusion.41 = (f32[2,516,1023]{2,1,0:T(8,128)S(1)}, f32[2,516,1023]{2,1,0:T(8,128)S(1)}) fusion(f32[2,518,1024]{2,1,0:T(8,128)S(1)} %maximum_convert_fusion), kind=kLoop, calls=%fused_computation.92 | loop fusion | bytes 16891776 | tf_op jit(solution)/shard_map/slice | solution.py:58
  62.9 2.5 %fusion.7 = f32[2,516,1024]{2,1,0:T(8,128)S(1)} fusion(f32[2,518,1024]{2,1,0:T(8,128)S(1)} %maximum_convert_fusion, f32[2,516,1023]{2,1,0:T(8,128)S(1)} %get-tuple-element.14, f32[2,516,1023]{2,1,0:T(8,128)S(1)} %get-tuple-element.13, f32[516]{0:T(1024)S(1)} %slice_multiply_fusion.4), kind=kLoop, calls=%fused_computation.10 | loop fusion | flops 6340608 | bytes 25356240 | tf_op jit(solution)/shard_map/mul | solution.py:132
  65.4 2.2 %fusion.40 = (f32[2,514,1023]{2,1,0:T(8,128)S(1)}, f32[2,514,1023]{2,1,0:T(8,128)S(1)}) fusion(f32[2,516,1024]{2,1,0:T(8,128)S(1)} %fusion.7), kind=kLoop, calls=%fused_computation.91 | loop fusion | bytes 16826304 | tf_op jit(solution)/shard_map/slice | solution.py:58
  67.6 2.6 %fusion.3 = f32[2,514,1024]{2,1,0:T(8,128)S(1)} fusion(f32[2,516,1024]{2,1,0:T(8,128)S(1)} %fusion.7, f32[2,518,1024]{2,1,0:T(8,128)S(1)} %maximum_convert_fusion, f32[2,514,1023]{2,1,0:T(8,128)S(1)} %get-tuple-element.12, f32[2,514,1023]{2,1,0:T(8,128)S(1)} %get-tuple-element.11, f32[514]{0:T(1024)S(1)} %slice_multiply_fusion.3), kind=kLoop, calls=%fused_computation.5 | loop fusion | flops 6316032 | bytes 25257960 | tf_op jit(solution)/shard_map/mul | solution.py:132
  70.2 2.1 %fusion.39 = (f32[2,512,1023]{2,1,0:T(8,128)S(1)}, f32[2,512,1023]{2,1,0:T(8,128)S(1)}) fusion(f32[2,514,1024]{2,1,0:T(8,128)S(1)} %fusion.3), kind=kLoop, calls=%fused_computation.90 | loop fusion | bytes 16760832 | tf_op jit(solution)/shard_map/slice | solution.py:58
  72.3 3.5 %fusion.14 = bf16[1,2,512,1024]{3,2,1,0:T(8,128)(2,1)} fusion(f32[512]{0:T(512)S(1)} %slice_multiply_fusion.5, f32[2,512,1023]{2,1,0:T(8,128)S(1)} %get-tuple-element.10, f32[2,512,1023]{2,1,0:T(8,128)S(1)} %get-tuple-element.9, f32[2,514,1024]{2,1,0:T(8,128)S(1)} %fusion.3, f32[2,518,1024]{2,1,0:T(8,128)S(1)} %maximum_convert_fusion), kind=kLoop, calls=%fused_computation.24 | loop fusion | flops 7340032 | bytes 23062528 | tf_op jit(solution)/shard_map/broadcast_in_dim | solution.py:133
  (18 shorter events, 0.2 us)
Async XLA Ops:
  0.0 8.1 %copy-start = (bf16[1,8,2,16,1024]{4,3,2,1,0:T(8,128)(2,1)S(1)}, bf16[1,8,2,16,1024]{4,3,2,1,0:T(8,128)(2,1)}, u32[]{:S(2)}) copy-start(bf16[1,8,2,16,1024]{4,3,2,1,0:T(8,128)(2,1)} %param.6) | copy-start | bytes 1572868
  0.0 14.4 %copy-start.1 = (bf16[2,4,1024]{2,1,0:T(4,128)(2,1)S(1)}, bf16[2,4,1024]{2,1,0:T(4,128)(2,1)}, u32[]{:S(2)}) copy-start(bf16[2,4,1024]{2,1,0:T(4,128)(2,1)} %param.7) | copy-start | bytes 49156
  0.0 14.4 %copy-start.2 = (bf16[2,4,1024]{2,1,0:T(4,128)(2,1)S(1)}, bf16[2,4,1024]{2,1,0:T(4,128)(2,1)}, u32[]{:S(2)}) copy-start(bf16[2,4,1024]{2,1,0:T(4,128)(2,1)} %param.8) | copy-start | bytes 49156
  2.9 44.8 %collective-permute-start.5 = (bf16[1,2,2]{0,2,1:T(2,128)(2,1)S(1)}, bf16[1,2,2]{0,2,1:T(2,128)(2,1)S(1)}, u32[]{:S(2)}, u32[]{:S(2)}) collective-permute-start(bf16[1,2,2]{0,2,1:T(2,128)(2,1)S(1)} %get-tuple-element.20), channel_id=1, source_target_pairs={{0,24},{4,28},{8,0},{12,4},{16,8},{20,12},{24,16},{28,20},{1,25},{... | collective-permute-start | bytes 32 | tf_op jit(solution)/shard_map/ppermute | solution.py:101
  3.0 42.9 %collective-permute-start.2 = (bf16[1,2,2]{0,2,1:T(2,128)(2,1)S(1)}, bf16[1,2,2]{0,2,1:T(2,128)(2,1)S(1)}, u32[]{:S(2)}, u32[]{:S(2)}) collective-permute-start(bf16[1,2,2]{0,2,1:T(2,128)(2,1)S(1)} %get-tuple-element.21), channel_id=1, source_target_pairs={{0,12},{4,16},{8,20},{12,24},{16,28},{20,0},{24,4},{28,8},{1,13},{... | collective-permute-start | bytes 32 | tf_op jit(solution)/shard_map/ppermute | solution.py:101
  5.3 40.6 %collective-permute-start.3 = (bf16[1,2,2]{0,2,1:T(2,128)(2,1)S(1)}, bf16[1,2,2]{0,2,1:T(2,128)(2,1)S(1)}, u32[]{:S(2)}, u32[]{:S(2)}) collective-permute-start(bf16[1,2,2]{0,2,1:T(2,128)(2,1)S(1)} %get-tuple-element.22), channel_id=1, source_target_pairs={{0,16},{4,20},{8,24},{12,28},{16,0},{20,4},{24,8},{28,12},{1,17},{... | collective-permute-start | bytes 32 | tf_op jit(solution)/shard_map/ppermute | solution.py:101
  5.4 42.5 %collective-permute-start.6 = (bf16[1,2,2]{0,2,1:T(2,128)(2,1)S(1)}, bf16[1,2,2]{0,2,1:T(2,128)(2,1)S(1)}, u32[]{:S(2)}, u32[]{:S(2)}) collective-permute-start(bf16[1,2,2]{0,2,1:T(2,128)(2,1)S(1)} %get-tuple-element.17), channel_id=1, source_target_pairs={{0,28},{4,0},{8,4},{12,8},{16,12},{20,16},{24,20},{28,24},{1,29},{... | collective-permute-start | bytes 32 | tf_op jit(solution)/shard_map/ppermute | solution.py:101
  7.4 28.0 %collective-permute-start = (bf16[1,2,2]{0,2,1:T(2,128)(2,1)S(1)}, bf16[1,2,2]{0,2,1:T(2,128)(2,1)S(1)}, u32[]{:S(2)}, u32[]{:S(2)}) collective-permute-start(bf16[1,2,2]{0,2,1:T(2,128)(2,1)S(1)} %get-tuple-element.18), channel_id=1, source_target_pairs={{0,4},{4,8},{8,12},{12,16},{16,20},{20,24},{24,28},{28,0},{1,5},{5... | collective-permute-start | bytes 32 | tf_op jit(solution)/shard_map/ppermute | solution.py:101
  9.9 38.8 %all-to-all-start = ((bf16[16,2,16,1024]{3,2,1,0:T(8,128)(2,1)}), bf16[16,2,16,1024]{3,2,1,0:T(8,128)(2,1)S(1)}, u32[]{:S(2)}, u32[]{:S(2)}) async-start(bf16[16,2,16,1024]{3,2,1,0:T(8,128)(2,1)} %select_multiply_fusion), calls=%async_computation | async-start | bytes 2097152 | tf_op jit(solution)/shard_map/all_to_all | solution.py:107
  35.3 2.8 %collective-permute-start.1 = (bf16[1,2,2]{0,2,1:T(2,128)(2,1)S(1)}, bf16[1,2,2]{0,2,1:T(2,128)(2,1)S(1)}, u32[]{:S(2)}, u32[]{:S(2)}) collective-permute-start(bf16[1,2,2]{0,2,1:T(2,128)(2,1)S(1)} %get-tuple-element.19), channel_id=1, source_target_pairs={{0,8},{4,12},{8,16},{12,20},{16,24},{20,28},{24,0},{28,4},{1,9},{5... | collective-permute-start | bytes 32 | tf_op jit(solution)/shard_map/ppermute | solution.py:101
  38.1 9.3 %collective-permute-start.4 = (bf16[1,2,2]{0,2,1:T(2,128)(2,1)S(1)}, bf16[1,2,2]{0,2,1:T(2,128)(2,1)S(1)}, u32[]{:S(2)}, u32[]{:S(2)}) collective-permute-start(bf16[1,2,2]{0,2,1:T(2,128)(2,1)S(1)} %fusion.33), channel_id=1, source_target_pairs={{0,20},{4,24},{8,28},{12,0},{16,4},{20,8},{24,12},{28,16},{1,21},{... | collective-permute-start | bytes 32 | tf_op jit(solution)/shard_map/ppermute | solution.py:101
  49.6 6.7 %collective-permute-start.7 = (bf16[2,3,1024]{2,1,0:T(4,128)(2,1)S(1)}, bf16[2,3,1024]{2,1,0:T(4,128)(2,1)S(1)}, u32[]{:S(2)}, u32[]{:S(2)}) collective-permute-start(bf16[2,3,1024]{2,1,0:T(4,128)(2,1)S(1)} %get-tuple-element.15), channel_id=1, source_target_pairs={{0,4},{4,8},{8,12},{12,16},{16,20},{20,24},{24,28},{1,5},{5,9},{9,... | collective-permute-start | bytes 36872 | tf_op jit(solution)/shard_map/ppermute | solution.py:34
  54.2 6.0 %collective-permute-start.8 = (bf16[2,3,1024]{2,1,0:T(4,128)(2,1)S(1)}, bf16[2,3,1024]{2,1,0:T(4,128)(2,1)S(1)}, u32[]{:S(2)}, u32[]{:S(2)}) collective-permute-start(bf16[2,3,1024]{2,1,0:T(4,128)(2,1)S(1)} %get-tuple-element.16), channel_id=1, source_target_pairs={{4,0},{8,4},{12,8},{16,12},{20,16},{24,20},{28,24},{5,1},{9,5},{13... | collective-permute-start | bytes 36872 | tf_op jit(solution)/shard_map/ppermute | solution.py:36
